TPU v7x, 32 devices: a whole 2x2x4 slice. The times are simulated.
32 devices in a mesh: seq: 16 (over z, x, core), exp: 2 (over y).
Axes of the slice: x: 2, y: 2, z: 4, core: 2. Of those that a mesh axis runs over, the one named last changes fastest.
Arguments:
- tokens: bfloat16 [30720, 1024], P('seq'), may hold values from -24 to 24
- slot_embed: bfloat16 [1024, 512], P(None, 'exp'), may hold values from -3 to 3
- w_in: bfloat16 [32, 1024, 4096], P('exp', None, 'seq'), may hold values from -0.375 to 0.375
- w_out: bfloat16 [32, 4096, 1024], P('exp', 'seq'), may hold values from -0.125 to 0.125
Outputs:
- mixed_out: bfloat16 [30720, 1024], P('seq', 'exp')
All inputs are finite; a program needn't handle non-finite values.
Results may differ from a plain program's by a relative error of at most 0.012.
Values may be sent and summed in bfloat16 or wider, within the bound.
A program may use at most 64 MiB of HBM per device.

v0:
```python
import jax
import jax.numpy as jnp
from jax import lax
from jax.sharding import PartitionSpec as P


def joined(part, axis, combine):
    gathered = jax.tree.map(lambda a: lax.all_gather(a, axis), part)

    def take(source):
        return jax.tree.map(lambda a: lax.dynamic_index_in_dim(a, source, 0, False), gathered)

    return lax.fori_loop(
        1, lax.axis_size(axis), lambda source, state: combine(state, take(source)), take(0)
    )


def gelu_tanh(values):
    return (
        0.5
        * values
        * (1.0 + jnp.tanh(0.7978845608028654 * (values + 0.044715 * values * values * values)))
    )


def pair_max(earlier, later):
    peak = jnp.maximum(earlier[0], later[0])
    return (peak, earlier[1] * jnp.exp(earlier[0] - peak) + later[1] * jnp.exp(later[0] - peak))


def on_device(tokens, slot_embed, w_in, w_out):
    experts_here = w_in.shape[0]
    slot_count = slot_embed.shape[1]
    slot_exp = slot_count // experts_here
    features = tokens.shape[1]
    logits = jnp.dot(tokens, slot_embed, preferred_element_type=jnp.float32)
    col_peak = jnp.max(logits, axis=0)
    local_weights = jnp.exp(logits - col_peak[None, :])
    peak_all, total_all = joined((col_peak, jnp.sum(local_weights, axis=0)), "seq", pair_max)
    weights = local_weights * jnp.exp(col_peak - peak_all)[None, :]
    dispatch = (weights / total_all[None, :]).astype(jnp.bfloat16)
    partial_in = lax.dot_general(
        dispatch, tokens, (((0,), (0,)), ((), ())), preferred_element_type=jnp.float32
    )
    slot_in = lax.psum(partial_in, "seq").astype(jnp.bfloat16)
    grouped = slot_in.reshape(experts_here, slot_exp, features)
    hidden = gelu_tanh(
        jnp.einsum("esd,edh->esh", grouped, w_in, preferred_element_type=jnp.float32)
    ).astype(jnp.bfloat16)
    partial_out = jnp.einsum(
        "esh,ehd->esd", hidden, w_out, preferred_element_type=jnp.float32
    ).reshape(slot_count, features)
    slot_out = lax.psum(partial_out, "seq").astype(jnp.bfloat16)
    row_peak = lax.pmax(jnp.max(logits, axis=1), "exp")
    row_weights = jnp.exp(logits - row_peak[:, None])
    row_sum = lax.psum(jnp.sum(row_weights, axis=1), "exp")
    combine = (row_weights / row_sum[:, None]).astype(jnp.bfloat16)
    term = jnp.dot(combine, slot_out, preferred_element_type=jnp.float32)
    mixed_out = lax.psum_scatter(term.astype(jnp.bfloat16), "exp", scatter_dimension=1, tiled=True)
    return mixed_out


def solution(mesh):
    placed = (P("seq", None), P(None, "exp"), P("exp", None, "seq"), P("exp", "seq", None))
    return jax.shard_map(
        on_device, mesh=mesh, in_specs=placed, out_specs=P("seq", "exp"), check_vma=False
    )
```

profile of v0, /device:TPU:0, one launch (start us, length us, event | category | flops | bytes accessed | tf_op | source)
XLA Modules:
  0.0 275.3 jit_solution(14795030857905680253)
XLA Ops:
  6.5 0.0 copy-start
  6.5 0.0 reduce-scatter.2.cloned.1.call-start
  6.5 1.0 copy-done
  7.6 3.4 %fusion.24 = (f32[256]{0:T(256)S(1)}, f32[1920]{0:T(1024)S(1)}, f32[1920,256]{1,0:T(8,128)S(1)}) fusion(bf16[1920,1024]{1,0:T(8,128)(2,1)} %param.6, bf16[1024,256]{1,0:T(8,128)(2,1)S(1)} %copy-done), kind=kOutput, calls=%fused_computation.35 | convolution fusion | flops 1007613824 | bytes 6431232 | tf_op jit(solution)/shard_map/dot_general | solution.py:36
  11.0 0.0 copy-start.1
  11.0 6.0 %pmax.7 = f32[1920]{0:T(1024)S(1)} all-reduce(f32[1920]{0:T(1024)S(1)} %get-tuple-element.143), channel_id=1, replica_groups=mesh['seq'=16,'exp'=2] {'exp'}, use_global_device_ids=true, to_apply=%region_1.0 | all-reduce | flops 1920 | bytes 15360 | tf_op jit(solution)/shard_map/pmax | solution.py:54
  16.9 0.8 fusion.1
  17.7 22.2 %all-gather.3 = f32[16,1,256]{2,1,0:T(1,128)S(1)} all-gather(f32[1,1,256]{2,1,0:T(1,128)S(1)} %bitcast.34), channel_id=3, replica_groups=mesh['seq'=16,'exp'=2] {'seq'}, dimensions={0}, use_global_device_ids=true | all-gather | bytes 17408 | tf_op jit(solution)/shard_map/all_gather | solution.py:8
  39.9 17.4 %all-gather.2 = f32[16,1,256]{2,1,0:T(1,128)S(1)} all-gather(f32[1,1,256]{2,1,0:T(1,128)S(1)} %bitcast.33), channel_id=2, replica_groups=mesh['seq'=16,'exp'=2] {'seq'}, dimensions={0}, use_global_device_ids=true | all-gather | bytes 17408 | tf_op jit(solution)/shard_map/all_gather | solution.py:8
  57.3 5.6 %psum.21 = f32[1920]{0:T(1024)} all-reduce(f32[1920]{0:T(1024)S(1)} %get-tuple-element.141), channel_id=1, replica_groups=mesh['seq'=16,'exp'=2] {'exp'}, use_global_device_ids=true, to_apply=%region_3.4 | all-reduce | flops 1920 | bytes 15360 | tf_op jit(solution)/shard_map/psum | solution.py:56
  62.9 0.8 while.17
  63.7 0.0 copy-done.1
  63.8 3.4 %fusion.2 = f32[256,1024]{1,0:T(8,128)S(1)} fusion(bf16[1920,1024]{1,0:T(8,128)(2,1)} %param.6, f32[1920,256]{1,0:T(8,128)S(1)} %get-tuple-element.158, f32[256]{0:T(256)S(1)} %get-tuple-element.139, f32[256]{0:T(256)S(1)} %subtract_exponential_fusion.2, f32[256]{0:T(256)S(1)} %get-tuple-element.142), kind=kOutput, calls=%fused_computation.10 | convolution fusion | flops 1008599040 | bytes 6949888 | tf_op jit(solution)/shard_map/dot_general | solution.py:42
  67.2 69.7 %all-reduce.2 = bf16[256,1024]{1,0:T(8,128)(2,1)S(1)} all-reduce(f32[256,1024]{1,0:T(8,128)S(1)} %fusion.2), channel_id=1, replica_groups=mesh['seq'=16,'exp'=2] {'seq'}, use_global_device_ids=true, to_apply=%region_8.9 | all-reduce | flops 262144 | bytes 1572864 | tf_op jit(solution)/shard_map/psum | solution.py:45
  136.8 0.0 copy-start.2
  136.8 8.1 %fusion.14 = f32[16,16,1024]{2,1,0:T(8,128)S(1)} fusion(bf16[16,256,1024]{2,1,0:T(8,128)(2,1)} %param.9, bf16[16,16,1024]{2,1,0:T(8,128)(2,1)S(1)} %bitcast.26, bf16[16,1024,256]{2,1,0:T(8,128)(2,1)} %param.8), kind=kOutput, calls=%fused_computation.23 | convolution fusion | flops 269025280 | bytes 18350080 | tf_op jit(solution)/shard_map/esh,ehd->esd/dot_general | solution.py:50
  144.9 69.3 %all-reduce.3 = bf16[256,1024]{1,0:T(8,128)(2,1)S(1)} all-reduce(f32[256,1024]{1,0:T(8,128)S(1)} %bitcast.25), channel_id=1, replica_groups=mesh['seq'=16,'exp'=2] {'seq'}, use_global_device_ids=true, to_apply=%region_9.10 | all-reduce | flops 262144 | bytes 1572864 | tf_op jit(solution)/shard_map/psum | solution.py:53
  214.2 0.0 copy-done.2
  214.2 4.7 %convolution_convert_fusion = bf16[1920,1024]{1,0:T(8,128)(2,1)} fusion(f32[1920,256]{1,0:T(8,128)} %copy-done.1, f32[1920]{0:T(1024)S(1)} %copy-done.2, f32[1920]{0:T(1024)S(1)} %pmax.7, bf16[256,1024]{1,0:T(8,128)(2,1)S(1)} %all-reduce.3), kind=kOutput, calls=%fused_computation.3 | convolution fusion | flops 1010073600 | bytes 6437888 | tf_op jit(solution)/shard_map/dot_general | solution.py:58
  218.9 0.0 reduce-scatter.2.cloned.1.call-update
  219.0 49.5 %reduce-scatter.2.cloned.1.call-done = bf16[1920,512]{1,0:T(8,128)(2,1)} async-done(((bf16[1920,1024]{1,0:T(8,128)(2,1)}), bf16[1920,512]{1,0:T(8,128)(2,1)}) %reduce-scatter.2.cloned.1.call-update) | async-done | bytes 1966096 | tf_op jit(solution)/shard_map/reduce_scatter | solution.py:59
  (35 shorter events, 0.5 us)
Async XLA Ops:
  6.5 1.0 copy-start
  6.5 261.9 %reduce-scatter.2.cloned.1.call-start = ((), (), s32[]{:S(2)}) async-start(), calls=%async_computation.1 | async-start | bytes 5898240 | tf_op jit(solution)/shard_map/reduce_scatter | solution.py:59
  11.0 52.8 %copy-start.1 = (f32[1920,256]{1,0:T(8,128)}, f32[1920,256]{1,0:T(8,128)S(1)}, u32[]{:S(2)}) copy-start(f32[1920,256]{1,0:T(8,128)S(1)} %get-tuple-element.158) | copy-start | bytes 5898244
  136.8 77.4 %copy-start.2 = (f32[1920]{0:T(1024)S(1)}, f32[1920]{0:T(1024)}, u32[]{:S(2)}) copy-start(f32[1920]{0:T(1024)} %psum.21) | copy-start | bytes 23044
Sparse Core Ops, SparseCore 0:
  219.1 49.3 reduce-scatter.1
where the time goes:
time: 276 us; the launch traced here: 275 us
  blocking collectives  190 us (69%)
  waiting for transfers between devices  49.5 us (18%)
  matrix products  19.6 us (7%)
  between operations  13.5 us (5%)
    psum x1, blocking collectives, on_device(): slot_in = lax.psum(partial_in, 'seq').astype(jnp.bfloat16)  69.7 us
    psum x1, blocking collectives, on_device(): slot_out = lax.psum(partial_out, 'seq').astype(jnp.bfloat16)  69.3 us
    reduce_scatter x1, waiting for transfers between devices, on_device(): lax.psum_scatter(term.astype(jnp.bfloat16), 'exp', scatter_dimension=1, t...  49.5 us
    all_gather x2, blocking collectives, joined(): gathered = jax.tree.map(lambda a: lax.all_gather(a, axis), part)  39.6 us
    dot_general x1, matrix products, on_device(): jnp.einsum('esh,ehd->esd', hidden, w_out, preferred_element_type=jnp.floa...  8.06 us
    pmax x1, blocking collectives, on_device(): row_peak = lax.pmax(jnp.max(logits, axis=1), 'exp')  5.97 us
    psum x1, blocking collectives, on_device(): row_sum = lax.psum(jnp.sum(row_weights, axis=1), 'exp')  5.56 us
  transfers between devices with their start and end apart: 1, of which 1 were waited for; matrix products, arithmetic and copies ran while one was open for 0% of the time, Pallas kernels for 0%

commit v1 on v0

v1 whole, which is shorter than its diff:
```python
import functools

import jax
import jax.numpy as jnp
from jax import lax
from jax.experimental import pallas as pl
from jax.experimental.pallas import tpu as pltpu
from jax.sharding import PartitionSpec as P

MESH = pl.DeviceIdType.MESH
F32 = jnp.float32
BF16 = jnp.bfloat16


def gelu_tanh(v):
    return 0.5 * v * (1.0 + jnp.tanh(0.7978845608028654 * (v + 0.044715 * v * v * v)))


def rcopy(src, dst, send, recv, dev):
    return pltpu.make_async_remote_copy(
        src_ref=src, dst_ref=dst, send_sem=send, recv_sem=recv, device_id=dev, device_id_type=MESH
    )


def column(row, slots):
    return jnp.transpose(jnp.broadcast_to(row, (128, slots)))


def kernel(
    n_seq, n_exp, slot_exp, tok_hbm, emb_hbm, win_hbm, wout_hbm, comb_hbm, so_hbm,
    tok, emb, embt, win, wout, logt, pt, acc, comb, mst, lst, tot,
    snd1, rcv1, snd2, rcv2, ag, keep, snd3, rcv3, snd4, rcv4, ybuf, so,
    sem_tok, sem_in, sem_w, sem_out, sem_emb, sem_m, sem_l,
    sem_1, sem_2, sem_ag, sem_fw, sem_3, sem_4, sem_y, sem_a, sem_af, sem_b, sem_bf,
):
    n_chip = n_seq // 2
    count, features = tok.shape
    slots = embt.shape[0]
    experts = win.shape[0]
    rows = slots // n_seq
    half = slots // 2
    cols = features // n_exp
    tile = 256
    n_tile = features // tile
    me = lax.axis_index("seq")
    mine = lax.axis_index("exp")
    chip = me // 2
    core = lax.rem(me, 2)
    other = 1 - core
    partner = {"seq": chip * 2 + other}
    pending = []

    def chip_at(r):
        return lax.rem(chip + r, n_chip)

    def chip_from(r):
        return lax.rem(chip - r + n_chip, n_chip)

    def seq_at(r):
        return {"seq": lax.rem(me + r, n_seq)}

    def exp_at(r):
        return {"exp": lax.rem(mine + r, n_exp)}

    def go(cp):
        cp.start()
        pending.append(cp)

    barrier = pltpu.get_barrier_semaphore()
    for r in range(1, n_seq):
        pl.semaphore_signal(barrier, inc=1, device_id=seq_at(r), device_id_type=MESH)
    for r in range(1, n_exp):
        pl.semaphore_signal(barrier, inc=1, device_id=exp_at(r), device_id_type=MESH)

    emb_in = pltpu.make_async_copy(emb_hbm, emb.at[0], sem_in)
    emb_in.start()
    chunks = []
    at = 0
    while at < count:
        size = min(512, count - at)
        cp = pltpu.make_async_copy(tok_hbm.at[pl.ds(at, size)], tok.at[pl.ds(at, size)], sem_tok.at[len(chunks)])
        cp.start()
        chunks.append((at, size, cp))
        at += size
    win_in = pltpu.make_async_copy(win_hbm, win, sem_w.at[0])
    wout_in = pltpu.make_async_copy(wout_hbm, wout, sem_w.at[1])
    win_in.start()
    wout_in.start()

    emb_in.wait()
    for q in range(n_tile):
        embt[:, q * tile:(q + 1) * tile] = jnp.transpose(emb[0, q * tile:(q + 1) * tile, :])
    peak = None
    for at, size, cp in chunks:
        cp.wait()
        lt = lax.dot_general(
            embt[...], tok[at:at + size, :], (((1,), (1,)), ((), ())), preferred_element_type=F32
        )
        logt[:, at:at + size] = lt
        top = jnp.max(lt, axis=1, keepdims=True)
        peak = top if peak is None else jnp.maximum(peak, top)
    peak_wide = jnp.broadcast_to(peak, (slots, 128))
    mst[0] = jnp.transpose(peak_wide)[0:8, :]

    pl.semaphore_wait(barrier, n_seq - 1 + n_exp - 1)
    stat_m = [rcopy(mst.at[0], mst.at[r], sem_m.at[0, r], sem_m.at[1, r], seq_at(r)) for r in range(1, n_seq)]
    for cp in stat_m:
        go(cp)
    embs = [rcopy(emb.at[0], emb.at[r], sem_emb.at[0, r], sem_emb.at[1, r], exp_at(r)) for r in range(1, n_exp)]
    for cp in embs:
        go(cp)

    total = None
    for at, size, _ in chunks:
        w = jnp.exp(logt[:, at:at + size] - peak)
        pt[:, at:at + size] = w.astype(BF16)
        part = jnp.sum(w, axis=1, keepdims=True)
        total = part if total is None else total + part
    lst[0] = jnp.transpose(jnp.broadcast_to(total, (slots, 128)))[0:8, :]
    stat_l = [rcopy(lst.at[0], lst.at[r], sem_l.at[0, r], sem_l.at[1, r], seq_at(r)) for r in range(1, n_seq)]
    for cp in stat_l:
        go(cp)

    for q in range(n_tile):
        acc[:, q * tile:(q + 1) * tile] = jnp.dot(
            pt[...], tok[:, q * tile:(q + 1) * tile], preferred_element_type=F32
        )
    for cp in stat_m:
        cp.wait_recv()
    top_all = jnp.max(mst[...], axis=0)
    scale = column(jnp.exp(mst[0] - top_all)[0:1, :], slots)[:, 0:1]

    def half_rows(which):
        return pl.ds(pl.multiple_of(which * half, half), half)

    acc[...] = acc[...] * scale
    first = []
    for q in range(n_tile):
        snd1[q] = acc[half_rows(other), q * tile:(q + 1) * tile].astype(BF16)
        cp = rcopy(snd1.at[q], rcv1.at[q], sem_1.at[0, q], sem_1.at[1, q], partner)
        go(cp)
        first.append(cp)
    for q in range(n_tile):
        first[q].wait_recv()
        both = acc[half_rows(core), q * tile:(q + 1) * tile] + rcv1[q].astype(F32)
        snd2[:, :, q * tile:(q + 1) * tile] = both.reshape(n_chip, rows, tile).astype(BF16)
    second = []
    for r in range(1, n_chip):
        to = chip_at(r)
        cp = rcopy(snd2.at[to], rcv2.at[r], sem_2.at[0, r], sem_2.at[1, r], {"seq": to * 2 + core})
        go(cp)
        second.append(cp)

    for cp in embs:
        cp.wait_recv()
    step = next(s for s in (384, 256, 128, 64, 32, 16) if count % s == 0)

    def combine(i, carry):
        here = pl.ds(pl.multiple_of(i * step, step), step)
        rows_in = tok[here, :]
        parts = [jnp.dot(rows_in, emb[r], preferred_element_type=F32) for r in range(n_exp)]
        top = jnp.max(functools.reduce(jnp.maximum, parts), axis=1, keepdims=True)
        parts = [jnp.exp(v - top) for v in parts]
        full = jnp.sum(functools.reduce(jnp.add, parts), axis=1, keepdims=True)
        inv = 1.0 / full
        for r in range(n_exp):
            comb[here, r * slots:(r + 1) * slots] = (parts[r] * inv).astype(BF16)
        return carry

    lax.fori_loop(0, count // step, combine, 0)
    comb_out = pltpu.make_async_copy(comb, comb_hbm, sem_out.at[0])
    comb_out.start()

    for cp in stat_l:
        cp.wait_recv()
    grand = jnp.sum(lst[...] * jnp.exp(mst[...] - top_all[None]), axis=0)
    tot[...] = column(grand[0:1, :], slots)
    piece = core * n_chip + chip
    mine_sum = snd2[chip].astype(F32)
    for r in range(1, n_chip):
        second[r - 1].wait_recv()
        mine_sum = mine_sum + rcv2[r].astype(F32)
    total_here = tot[pl.ds(pl.multiple_of(piece * rows, rows), rows), :][:, 0:1]
    ag[piece] = (mine_sum / total_here).astype(BF16)

    for r in range(1, n_chip):
        go(rcopy(ag.at[piece], ag.at[piece], sem_ag.at[0, r], sem_ag.at[1, r], {"seq": chip_at(r) * 2 + core}))
    go(rcopy(ag.at[piece], ag.at[piece], sem_fw.at[0, 0], sem_fw.at[1, 0], partner))
    win_in.wait()
    wout_in.wait()

    def expert(p):
        e = (p * rows) // slot_exp
        h = gelu_tanh(jnp.dot(ag[p], win[e], preferred_element_type=F32)).astype(BF16)
        return jnp.dot(h, wout[e], preferred_element_type=F32)

    group = 4
    for start in range(0, n_chip, group):
        rs = range(start, start + group)
        for r in rs:
            p = core * n_chip + chip_from(r)
            if r:
                rcopy(ag.at[p], ag.at[p], sem_ag.at[0, r], sem_ag.at[1, r], partner).wait_recv()
                go(rcopy(ag.at[p], ag.at[p], sem_fw.at[0, r], sem_fw.at[1, r], partner))
        for r in rs:
            keep[chip_from(r)] = expert(core * n_chip + chip_from(r))
    for start in range(0, n_chip, group):
        rs = range(start, start + group)
        for r in rs:
            p = other * n_chip + chip_from(r)
            rcopy(ag.at[p], ag.at[p], sem_fw.at[0, r], sem_fw.at[1, r], partner).wait_recv()
        for r in rs:
            snd3[r] = expert(other * n_chip + chip_from(r)).astype(BF16)
        for r in rs:
            go(rcopy(snd3.at[r], rcv3.at[r], sem_3.at[0, r], sem_3.at[1, r], partner))
    for r in range(n_chip):
        rcopy(snd3.at[r], rcv3.at[r], sem_3.at[0, r], sem_3.at[1, r], partner).wait_recv()
        owner = chip_from(r)
        snd4[r] = (keep[owner] + rcv3[r].astype(F32)).astype(BF16)
        if r:
            go(rcopy(snd4.at[r], rcv4.at[r], sem_4.at[0, r], sem_4.at[1, r], {"seq": owner * 2 + core}))
    final = snd4[0].astype(F32)
    for r in range(1, n_chip):
        rcopy(snd4.at[r], rcv4.at[r], sem_4.at[0, r], sem_4.at[1, r], partner).wait_recv()
        final = final + rcv4[r].astype(F32)
    final = final.astype(BF16)
    for q in range(n_exp):
        ybuf[q] = final[:, q * cols:(q + 1) * cols]
    for r in range(1, n_exp):
        go(rcopy(ybuf.at[lax.rem(mine + r, n_exp)], so.at[r, piece], sem_y.at[0, r], sem_y.at[1, r], exp_at(r)))
    so[0, piece] = ybuf[mine]

    def spread(span, sem_d, sem_r):
        def at_piece(p):
            return so.at[span, p]

        for r in range(1, n_chip):
            go(rcopy(at_piece(piece), at_piece(piece), sem_d.at[0, r], sem_d.at[1, r], {"seq": chip_at(r) * 2 + core}))
        go(rcopy(at_piece(piece), at_piece(piece), sem_r.at[0, 0], sem_r.at[1, 0], partner))

    def relay(span, sem_d, sem_r):
        for r in range(1, n_chip):
            p = core * n_chip + chip_from(r)
            rcopy(so.at[span, p], so.at[span, p], sem_d.at[0, r], sem_d.at[1, r], partner).wait_recv()
            go(rcopy(so.at[span, p], so.at[span, p], sem_r.at[0, r], sem_r.at[1, r], partner))

    def finish(span, sem_r):
        for r in range(n_chip):
            p = other * n_chip + chip_from(r)
            rcopy(so.at[span, p], so.at[span, p], sem_r.at[0, r], sem_r.at[1, r], partner).wait_recv()

    near = pl.ds(0, 1)
    far = pl.ds(1, n_exp - 1)
    spread(near, sem_a, sem_af)
    for r in range(1, n_exp):
        rcopy(ybuf.at[0], so.at[r, piece], sem_y.at[0, r], sem_y.at[1, r], exp_at(r)).wait_recv()
    spread(far, sem_b, sem_bf)
    relay(near, sem_a, sem_af)
    relay(far, sem_b, sem_bf)
    finish(near, sem_af)
    finish(far, sem_bf)
    so_out = pltpu.make_async_copy(so, so_hbm, sem_out.at[1])
    so_out.start()
    for cp in pending:
        cp.wait_send()
    comb_out.wait()
    so_out.wait()


def solution(mesh):
    n_seq, n_exp = mesh.shape["seq"], mesh.shape["exp"]
    n_chip = n_seq // 2

    def on_device(tokens, slot_embed, w_in, w_out):
        count, features = tokens.shape
        slots = slot_embed.shape[1]
        experts, _, hid = w_in.shape
        slot_exp = slots // experts
        rows = slots // n_seq
        half = slots // 2
        cols = features // n_exp
        n_tile = features // 256
        dma = pltpu.SemaphoreType.DMA
        vmem = pltpu.VMEM
        anywhere = pl.BlockSpec(memory_space=pl.ANY)
        comb, so = pl.pallas_call(
            functools.partial(kernel, n_seq, n_exp, slot_exp),
            out_shape=(
                jax.ShapeDtypeStruct((count, n_exp * slots), BF16),
                jax.ShapeDtypeStruct((n_exp, n_seq, rows, cols), BF16),
            ),
            in_specs=[anywhere] * 4,
            out_specs=(anywhere, anywhere),
            scratch_shapes=[
                vmem((count, features), BF16),
                vmem((n_exp, features, slots), BF16),
                vmem((slots, features), BF16),
                vmem(w_in.shape, BF16),
                vmem(w_out.shape, BF16),
                vmem((slots, count), F32),
                vmem((slots, count), BF16),
                vmem((slots, features), F32),
                vmem((count, n_exp * slots), BF16),
                vmem((n_seq, 8, slots), F32),
                vmem((n_seq, 8, slots), F32),
                vmem((slots, 128), F32),
                vmem((n_tile, half, 256), BF16),
                vmem((n_tile, half, 256), BF16),
                vmem((n_chip, rows, features), BF16),
                vmem((n_chip, rows, features), BF16),
                vmem((n_seq, rows, features), BF16),
                vmem((n_chip, rows, features), F32),
                vmem((n_chip, rows, features), BF16),
                vmem((n_chip, rows, features), BF16),
                vmem((n_chip, rows, features), BF16),
                vmem((n_chip, rows, features), BF16),
                vmem((n_exp, rows, cols), BF16),
                vmem((n_exp, n_seq, rows, cols), BF16),
                dma((-(-count // 512),)),
                dma,
                dma((2,)),
                dma((2,)),
                dma((2, n_exp)),
                dma((2, n_seq)),
                dma((2, n_seq)),
                dma((2, n_tile)),
                dma((2, n_chip)),
                dma((2, n_chip)),
                dma((2, n_chip)),
                dma((2, n_chip)),
                dma((2, n_chip)),
                dma((2, n_exp)),
                dma((2, n_chip)),
                dma((2, n_chip)),
                dma((2, n_chip)),
                dma((2, n_chip)),
            ],
            compiler_params=pltpu.CompilerParams(
                collective_id=0, has_side_effects=True, vmem_limit_bytes=60 * 1024 * 1024
            ),
        )(tokens, slot_embed, w_in, w_out)
        so = so.reshape(n_exp * slots, cols)
        return jnp.dot(comb, so, preferred_element_type=F32).astype(BF16)

    placed = (P("seq", None), P(None, "exp"), P("exp", None, "seq"), P("exp", "seq", None))
    return jax.shard_map(
        on_device, mesh=mesh, in_specs=placed, out_specs=P("seq", "exp"), check_vma=False
    )
```

time: 276 us -> 60.2 us (0.22)
  blocking collectives: 190 us -> 0 us
  Pallas kernels: 0 us -> 55.9 us
  waiting for transfers between devices: 49.5 us -> 0 us
  matrix products: 19.6 us -> 4.09 us
  between operations: 13.5 us -> 0.01 us
    psum x3 -> x0, blocking collectives: 144 us -> none  [the longest x1 69.7 us: on_device(): slot_in = lax.psum(partial_in, 'seq').astype(jnp.bfloat16)]
    pallas_call x0 -> x1, Pallas kernels: none -> 55.9 us  [on_device(): pl.pallas_call(functools.partial(kernel, n_seq, n_exp, slot_exp), out_sha...]
    reduce_scatter x1 -> x0, waiting for transfers between devices: 49.5 us -> none  [on_device(): lax.psum_scatter(term.astype(jnp.bfloat16), 'exp', scatter_dimension=1, t...]
    all_gather x2 -> x0, blocking collectives: 39.6 us -> none  [joined(): gathered = jax.tree.map(lambda a: lax.all_gather(a, axis), part)]
    dot_general x4 -> x1, matrix products: 19.6 us -> 4.09 us  [on_device(): return jnp.dot(comb, so, preferred_element_type=F32).astype(BF16)]
    pmax x1 -> x0, blocking collectives: 5.97 us -> none  [on_device(): row_peak = lax.pmax(jnp.max(logits, axis=1), 'exp')]
  transfers between devices with their start and end apart: 1 -> 0, of which waited for: 1 -> 0; matrix products, arithmetic and copies ran while one was open for 0% -> 0% of each run, Pallas kernels for 0% -> 0%
where the time goes in v1:
time: 60.2 us; the launch traced here: 60 us
  Pallas kernels  55.9 us (93%)
  matrix products  4.09 us (7%)
    pallas_call x1, Pallas kernels, on_device(): pl.pallas_call(functools.partial(kernel, n_seq, n_exp, slot_exp), out_sha...  55.9 us
    dot_general x1, matrix products, on_device(): return jnp.dot(comb, so, preferred_element_type=F32).astype(BF16)  4.09 us

profile of v1, /device:TPU:0, one launch (start us, length us, event | category | flops | bytes accessed | tf_op | source)
XLA Modules:
  0.0 60.0 jit_solution(12652899210280395105)
XLA Ops:
  0.0 55.9 %shard_map.46 = (bf16[1920,512]{1,0:T(8,128)(2,1)}, bf16[2,16,16,512]{3,2,1,0:T(8,128)(2,1)}) custom-call(bf16[1920,1024]{1,0:T(8,128)(2,1)} %tok_hbm.1, bf16[1024,256]{1,0:T(8,128)(2,1)} %emb_hbm.1, bf16[16,1024,256]{2,1,0:T(8,128)(2,1)} %win_hbm.1, bf16[16,256,1024]{2,1,0:T(8,128)(2,1)} %wout_hbm.1), custom_call_target="tpu_custom_call" | custom-call | tf_op jit(solution)/shard_map/pallas_call | solution.py:286
  55.9 4.1 %convolution_convert_fusion = bf16[1920,512]{1,0:T(8,128)(2,1)} fusion(bf16[1920,512]{1,0:T(8,128)(2,1)} %get-tuple-element.7, bf16[512,512]{1,0:T(8,128)(2,1)} %bitcast.3), kind=kOutput, calls=%fused_computation | convolution fusion | flops 1007616000 | bytes 4456448 | tf_op jit(solution)/shard_map/dot_general | solution.py:343

commit v2 on v1

v2 whole, which is shorter than its diff:
```python
import functools

import jax
import jax.numpy as jnp
from jax import lax
from jax.experimental import pallas as pl
from jax.experimental.pallas import tpu as pltpu
from jax.sharding import PartitionSpec as P

MESH = pl.DeviceIdType.MESH
F32 = jnp.float32
BF16 = jnp.bfloat16


def gelu_tanh(v):
    return 0.5 * v * (1.0 + jnp.tanh(0.7978845608028654 * (v + 0.044715 * v * v * v)))


def rcopy(src, dst, send, recv, dev):
    return pltpu.make_async_remote_copy(
        src_ref=src, dst_ref=dst, send_sem=send, recv_sem=recv, device_id=dev, device_id_type=MESH
    )


def column(row, slots):
    return jnp.transpose(jnp.broadcast_to(row, (128, slots)))


def kernel(
    n_seq, n_exp, slot_exp, tok_hbm, emb_hbm, win_hbm, wout_hbm, comb_hbm, so_hbm,
    tok, emb, embt, win, wout, logt, pt, acc, comb, m1, l1, s2, wide, tot,
    snd1, rcv1, snd2, rcv2, ag, keep, snd3, rcv3, snd4, rcv4, so,
    sem_tok, sem_in, sem_w, sem_out, sem_emb, sem_er, sem_m, sem_s,
    sem_1, sem_2, sem_ag, sem_fw, sem_3, sem_4, sem_a, sem_af,
):
    n_chip = n_seq // 2
    count, features = tok.shape
    slots = embt.shape[0]
    rows = slots // n_seq
    half = slots // 2
    cols = features // n_exp
    tile = 256
    n_tile = features // tile
    me = lax.axis_index("seq")
    mine = lax.axis_index("exp")
    chip = me // 2
    core = lax.rem(me, 2)
    other = 1 - core
    partner = {"seq": chip * 2 + other}
    pending = []

    def near(r):
        return chip_ids[r]

    chip_ids = [chip]
    for r in range(1, n_chip):
        mate, bit = chip, 1
        while bit < n_chip:
            if r & bit:
                mate = mate + bit * (1 - 2 * lax.rem(chip // bit, 2))
            bit *= 2
        chip_ids.append(mate)

    def peer(r):
        return {"seq": near(r) * 2 + core}

    def group_at(s):
        return lax.rem(mine + s, n_exp)

    def across(r, s):
        return {"seq": near(r) * 2 + core, "exp": group_at(s)}

    def go(cp):
        cp.start()
        pending.append(cp)

    barrier = pltpu.get_barrier_semaphore()
    for s in range(n_exp):
        for r in range(n_chip):
            if r or s:
                pl.semaphore_signal(barrier, inc=1, device_id=across(r, s), device_id_type=MESH)
    pl.semaphore_signal(barrier, inc=1, device_id=partner, device_id_type=MESH)

    emb_in = pltpu.make_async_copy(emb_hbm, emb.at[0], sem_in)
    emb_in.start()
    chunks = []
    at = 0
    while at < count:
        size = min(512, count - at)
        cp = pltpu.make_async_copy(tok_hbm.at[pl.ds(at, size)], tok.at[pl.ds(at, size)], sem_tok.at[len(chunks)])
        cp.start()
        chunks.append((at, size, cp))
        at += size

    emb_in.wait()
    for q in range(n_tile):
        embt[:, q * tile:(q + 1) * tile] = jnp.transpose(emb[0, q * tile:(q + 1) * tile, :])
    peak = None
    deep = features // 2

    def part_of(which):
        return pl.ds(pl.multiple_of(which * deep, deep), deep)

    def emb_copy(r):
        there = emb.at[r, part_of(core)]
        return rcopy(emb.at[0, part_of(core)], there, sem_emb.at[0, r], sem_emb.at[1, r], {"exp": group_at(r)})

    def emb_relay(r, which):
        there = emb.at[r, part_of(which)]
        return rcopy(there, there, sem_er.at[0, r], sem_er.at[1, r], partner)

    for at, size, cp in chunks:
        cp.wait()
        lt = lax.dot_general(
            embt[...], tok[at:at + size, :], (((1,), (1,)), ((), ())), preferred_element_type=F32
        )
        logt[:, at:at + size] = lt
        top = jnp.max(lt, axis=1, keepdims=True)
        peak = top if peak is None else jnp.maximum(peak, top)
        if at == 0:
            pl.semaphore_wait(barrier, n_chip * n_exp)
            for r in range(1, n_exp):
                go(emb_copy(r))
    win_in = pltpu.make_async_copy(win_hbm, win, sem_w.at[0])
    wout_in = pltpu.make_async_copy(wout_hbm, wout, sem_w.at[1])
    win_in.start()
    wout_in.start()
    m1[0] = jnp.transpose(jnp.broadcast_to(peak, (slots, 128)))[0:1, :]
    m_copy = rcopy(m1.at[0], m1.at[1], sem_m.at[0, 0], sem_m.at[1, 0], partner)
    go(m_copy)

    total = None
    for at, size, _ in chunks:
        w = jnp.exp(logt[:, at:at + size] - peak)
        pt[:, at:at + size] = w.astype(BF16)
        part = jnp.sum(w, axis=1, keepdims=True)
        total = part if total is None else total + part
    l1[0] = jnp.transpose(jnp.broadcast_to(total, (slots, 128)))[0:1, :]
    l_copy = rcopy(l1.at[0], l1.at[1], sem_m.at[0, 1], sem_m.at[1, 1], partner)
    go(l_copy)

    m_copy.wait_recv()
    top_pair = jnp.maximum(m1[0], m1[1])
    scale = column(jnp.exp(m1[0] - top_pair), slots)[:, 0:1]

    def half_rows(which):
        return pl.ds(pl.multiple_of(which * half, half), half)

    first = []
    for q in range(n_tile):
        acc[:, q * tile:(q + 1) * tile] = scale * jnp.dot(
            pt[...], tok[:, q * tile:(q + 1) * tile], preferred_element_type=F32
        )
        snd1[q] = acc[half_rows(other), q * tile:(q + 1) * tile].astype(BF16)
        cp = rcopy(snd1.at[q], rcv1.at[q], sem_1.at[0, q], sem_1.at[1, q], partner)
        go(cp)
        first.append(cp)
    l_copy.wait_recv()
    s2[0, 0] = top_pair
    s2[0, 1] = l1[0] * jnp.exp(m1[0] - top_pair) + l1[1] * jnp.exp(m1[1] - top_pair)
    stats = [rcopy(s2.at[0], s2.at[r], sem_s.at[0, r], sem_s.at[1, r], peer(r)) for r in range(1, n_chip)]
    for cp in stats:
        go(cp)
    for q in range(n_tile):
        first[q].wait_recv()
        both = acc[half_rows(core), q * tile:(q + 1) * tile] + rcv1[q].astype(F32)
        snd2[:, :, q * tile:(q + 1) * tile] = both.reshape(n_chip, rows, tile).astype(BF16)
    second = []
    for r in range(1, n_chip):
        cp = rcopy(snd2.at[near(r)], rcv2.at[r], sem_2.at[0, r], sem_2.at[1, r], peer(r))
        go(cp)
        second.append(cp)

    for r in range(1, n_exp):
        emb_copy(r).wait_recv()
        go(emb_relay(r, core))
    for r in range(1, n_exp):
        emb_relay(r, other).wait_recv()
    step = next(s for s in (384, 256, 128, 64, 32, 16) if count % s == 0)

    def combine(i, carry):
        here = pl.ds(pl.multiple_of(i * step, step), step)
        rows_in = tok[here, :]
        parts = [jnp.dot(rows_in, emb[r], preferred_element_type=F32) for r in range(n_exp)]
        top = jnp.max(functools.reduce(jnp.maximum, parts), axis=1, keepdims=True)
        parts = [jnp.exp(v - top) for v in parts]
        full = jnp.sum(functools.reduce(jnp.add, parts), axis=1, keepdims=True)
        inv = 1.0 / full
        for r in range(n_exp):
            comb[here, r * slots:(r + 1) * slots] = (parts[r] * inv).astype(BF16)
        return carry

    lax.fori_loop(0, count // step, combine, 0)
    comb_out = pltpu.make_async_copy(comb, comb_hbm, sem_out.at[0])
    comb_out.start()

    for cp in stats:
        cp.wait_recv()
    top_all = functools.reduce(jnp.maximum, [s2[r, 0] for r in range(n_chip)])
    factors = [jnp.exp(s2[r, 0] - top_all) for r in range(n_chip)]
    grand = functools.reduce(jnp.add, [s2[r, 1] * factors[r] for r in range(n_chip)])
    wide[...] = jnp.zeros_like(wide)
    for r in range(n_chip):
        wide[r:r + 1, :] = factors[r] / grand
    tot[...] = jnp.transpose(wide[...])
    piece = core * n_chip + chip
    weight = tot[pl.ds(pl.multiple_of(piece * rows, rows), rows), :]
    mine_sum = snd2[chip].astype(F32) * weight[:, 0:1]
    for r in range(1, n_chip):
        second[r - 1].wait_recv()
        mine_sum = mine_sum + rcv2[r].astype(F32) * weight[:, r:r + 1]
    ag[piece] = mine_sum.astype(BF16)

    go(rcopy(ag.at[piece], ag.at[piece], sem_fw.at[0, 0], sem_fw.at[1, 0], partner))
    for r in range(1, n_chip):
        go(rcopy(ag.at[piece], ag.at[piece], sem_ag.at[0, r], sem_ag.at[1, r], peer(r)))
    win_in.wait()
    wout_in.wait()

    def expert(p):
        e = (p * rows) // slot_exp
        h = gelu_tanh(jnp.dot(ag[p], win[e], preferred_element_type=F32)).astype(BF16)
        return jnp.dot(h, wout[e], preferred_element_type=F32)

    def flush(rs):
        for r in rs:
            rcopy(snd3.at[r], rcv3.at[r], sem_3.at[0, r], sem_3.at[1, r], partner).wait_recv()
            y = (keep[r] + rcv3[r].astype(F32)).astype(BF16)
            for q in range(n_exp):
                snd4[r, q] = y[:, q * cols:(q + 1) * cols]
            for s in range(n_exp):
                if r or s:
                    go(rcopy(snd4.at[r, group_at(s)], rcv4.at[s, r], sem_4.at[0, s, r], sem_4.at[1, s, r], across(r, s)))

    group = 4
    ready = None
    for start in range(0, n_chip, group):
        rs = range(start, min(start + group, n_chip))
        for r in rs:
            p = core * n_chip + near(r)
            if r:
                rcopy(ag.at[p], ag.at[p], sem_ag.at[0, r], sem_ag.at[1, r], partner).wait_recv()
                go(rcopy(ag.at[p], ag.at[p], sem_fw.at[0, r], sem_fw.at[1, r], partner))
        for r in rs:
            keep[r] = expert(core * n_chip + near(r))
        for r in rs:
            p = other * n_chip + near(r)
            rcopy(ag.at[p], ag.at[p], sem_fw.at[0, r], sem_fw.at[1, r], partner).wait_recv()
        for r in rs:
            snd3[r] = expert(other * n_chip + near(r)).astype(BF16)
        for r in rs:
            go(rcopy(snd3.at[r], rcv3.at[r], sem_3.at[0, r], sem_3.at[1, r], partner))
        if ready is not None:
            flush(ready)
        ready = rs
    flush(ready)
    for s in range(n_exp):
        sums = snd4[0, mine].astype(F32) if s == 0 else None
        for r in range(n_chip):
            if r or s:
                rcopy(snd4.at[0, 0], rcv4.at[s, r], sem_4.at[0, s, r], sem_4.at[1, s, r], partner).wait_recv()
                got = rcv4[s, r].astype(F32)
                sums = got if sums is None else sums + got
        so[s, piece] = sums.astype(BF16)

    every = pl.ds(0, n_exp)

    def so_copy(p, sems, r, dev):
        return rcopy(so.at[every, p], so.at[every, p], sems.at[0, r], sems.at[1, r], dev)

    go(so_copy(piece, sem_af, 0, partner))
    for r in range(1, n_chip):
        go(so_copy(piece, sem_a, r, peer(r)))
    for r in range(1, n_chip):
        p = core * n_chip + near(r)
        so_copy(p, sem_a, r, partner).wait_recv()
        go(so_copy(p, sem_af, r, partner))
    for r in range(n_chip):
        so_copy(other * n_chip + near(r), sem_af, r, partner).wait_recv()
    so_out = pltpu.make_async_copy(so, so_hbm, sem_out.at[1])
    so_out.start()
    for cp in pending:
        cp.wait_send()
    comb_out.wait()
    so_out.wait()


def mix_kernel(comb, so, out):
    out[...] = jnp.dot(comb[...], so[...], preferred_element_type=F32).astype(BF16)


def mix(comb, so):
    count, slots = comb.shape
    cols = so.shape[1]
    step = next(s for s in (384, 256, 128, 64, 32, 16) if count % s == 0)
    return pl.pallas_call(
        mix_kernel,
        out_shape=jax.ShapeDtypeStruct((count, cols), BF16),
        grid=(count // step,),
        in_specs=[
            pl.BlockSpec((step, slots), lambda i: (i, 0)),
            pl.BlockSpec((slots, cols), lambda i: (0, 0)),
        ],
        out_specs=pl.BlockSpec((step, cols), lambda i: (i, 0)),
    )(comb, so)


def solution(mesh):
    n_seq, n_exp = mesh.shape["seq"], mesh.shape["exp"]
    n_chip = n_seq // 2

    def on_device(tokens, slot_embed, w_in, w_out):
        count, features = tokens.shape
        slots = slot_embed.shape[1]
        experts, _, hid = w_in.shape
        slot_exp = slots // experts
        rows = slots // n_seq
        half = slots // 2
        cols = features // n_exp
        n_tile = features // 256
        dma = pltpu.SemaphoreType.DMA
        vmem = pltpu.VMEM
        anywhere = pl.BlockSpec(memory_space=pl.ANY)
        comb, so = pl.pallas_call(
            functools.partial(kernel, n_seq, n_exp, slot_exp),
            out_shape=(
                jax.ShapeDtypeStruct((count, n_exp * slots), BF16),
                jax.ShapeDtypeStruct((n_exp, n_seq, rows, cols), BF16),
            ),
            in_specs=[anywhere] * 4,
            out_specs=(anywhere, anywhere),
            scratch_shapes=[
                vmem((count, features), BF16),
                vmem((n_exp, features, slots), BF16),
                vmem((slots, features), BF16),
                vmem(w_in.shape, BF16),
                vmem(w_out.shape, BF16),
                vmem((slots, count), F32),
                vmem((slots, count), BF16),
                vmem((slots, features), F32),
                vmem((count, n_exp * slots), BF16),
                vmem((2, 1, slots), F32),
                vmem((2, 1, slots), F32),
                vmem((n_chip, 2, 1, slots), F32),
                vmem((128, slots), F32),
                vmem((slots, 128), F32),
                vmem((n_tile, half, 256), BF16),
                vmem((n_tile, half, 256), BF16),
                vmem((n_chip, rows, features), BF16),
                vmem((n_chip, rows, features), BF16),
                vmem((n_seq, rows, features), BF16),
                vmem((n_chip, rows, features), F32),
                vmem((n_chip, rows, features), BF16),
                vmem((n_chip, rows, features), BF16),
                vmem((n_chip, n_exp, rows, cols), BF16),
                vmem((n_exp, n_chip, rows, cols), BF16),
                vmem((n_exp, n_seq, rows, cols), BF16),
                dma((-(-count // 512),)),
                dma,
                dma((2,)),
                dma((2,)),
                dma((2, n_exp)),
                dma((2, n_exp)),
                dma((2, 2)),
                dma((2, n_chip)),
                dma((2, n_tile)),
                dma((2, n_chip)),
                dma((2, n_chip)),
                dma((2, n_chip)),
                dma((2, n_chip)),
                dma((2, n_exp, n_chip)),
                dma((2, n_chip)),
                dma((2, n_chip)),
            ],
            compiler_params=pltpu.CompilerParams(
                collective_id=0, has_side_effects=True, vmem_limit_bytes=60 * 1024 * 1024
            ),
        )(tokens, slot_embed, w_in, w_out)
        so = so.reshape(n_exp * slots, cols)
        return mix(comb, so)

    placed = (P("seq", None), P(None, "exp"), P("exp", None, "seq"), P("exp", "seq", None))
    return jax.shard_map(
        on_device, mesh=mesh, in_specs=placed, out_specs=P("seq", "exp"), check_vma=False
    )
```

time: 60.2 us -> 54.4 us (0.904); the launches traced: 60 us -> 53.5 us
  matrix products: 4.09 us -> 0 us
  Pallas kernels: 55.9 us -> 53.5 us
    pallas_call x1, Pallas kernels: 55.9 us -> 48.2 us  [on_device(): pl.pallas_call(functools.partial(kernel, n_seq, n_exp, slot_exp), out_sha...]
    pallas_call x0 -> x1, Pallas kernels: none -> 5.35 us  [mix(): pl.pallas_call(mix_kernel, out_shape=jax.ShapeDtypeStruct((count, cols),...]
    dot_general x1 -> x0, matrix products: 4.09 us -> none  [on_device(): return jnp.dot(comb, so, preferred_element_type=F32).astype(BF16)]
where the time goes in v2:
time: 54.4 us; the launch traced here: 53.5 us
  Pallas kernels  53.5 us (98%)
    pallas_call x1, Pallas kernels, on_device(): pl.pallas_call(functools.partial(kernel, n_seq, n_exp, slot_exp), out_sha...  48.2 us
    pallas_call x1, Pallas kernels, mix(): pl.pallas_call(mix_kernel, out_shape=jax.ShapeDtypeStruct((count, cols),...  5.35 us

profile of v2, /device:TPU:0, one launch (start us, length us, event | category | flops | bytes accessed | tf_op | source)
XLA Modules:
  0.0 53.5 jit_solution(944902073395369093)
XLA Ops:
  0.0 48.2 %shard_map.46 = (bf16[1920,512]{1,0:T(8,128)(2,1)}, bf16[2,16,16,512]{3,2,1,0:T(8,128)(2,1)}) custom-call(bf16[1920,1024]{1,0:T(8,128)(2,1)} %tok_hbm.1, bf16[1024,256]{1,0:T(8,128)(2,1)} %emb_hbm.1, bf16[16,1024,256]{2,1,0:T(8,128)(2,1)} %win_hbm.1, bf16[16,256,1024]{2,1,0:T(8,128)(2,1)} %wout_hbm.1), custom_call_target="tpu_custom_call" | custom-call | tf_op jit(solution)/shard_map/pallas_call | solution.py:324
  48.2 5.4 %shard_map.47 = bf16[1920,512]{1,0:T(8,128)(2,1)} custom-call(bf16[1920,512]{1,0:T(8,128)(2,1)} %get-tuple-element.7.comb, bf16[512,512]{1,0:T(8,128)(2,1)} %bitcast.1), custom_call_target="tpu_custom_call" | custom-call | tf_op jit(solution)/shard_map/pallas_call | solution.py:296

commit v3 on v2

--- a/solution.py
+++ b/solution.py
@@ -27,10 +27,10 @@
 
 
 def kernel(
-    n_seq, n_exp, slot_exp, tok_hbm, emb_hbm, win_hbm, wout_hbm, comb_hbm, so_hbm,
+    n_seq, n_exp, slot_exp, tok_hbm, emb_hbm, win_hbm, wout_hbm, out,
     tok, emb, embt, win, wout, logt, pt, acc, comb, m1, l1, s2, wide, tot,
     snd1, rcv1, snd2, rcv2, ag, keep, snd3, rcv3, snd4, rcv4, so,
-    sem_tok, sem_in, sem_w, sem_out, sem_emb, sem_er, sem_m, sem_s,
+    sem_tok, sem_in, sem_w, sem_emb, sem_er, sem_m, sem_s,
     sem_1, sem_2, sem_ag, sem_fw, sem_3, sem_4, sem_a, sem_af,
 ):
     n_chip = n_seq // 2
@@ -41,6 +41,8 @@
     cols = features // n_exp
     tile = 256
     n_tile = features // tile
+    n_cut = so.shape[0]
+    wide_cut = cols // n_cut
     me = lax.axis_index("seq")
     mine = lax.axis_index("exp")
     chip = me // 2
@@ -191,8 +193,6 @@
         return carry
 
     lax.fori_loop(0, count // step, combine, 0)
-    comb_out = pltpu.make_async_copy(comb, comb_hbm, sem_out.at[0])
-    comb_out.start()
 
     for cp in stats:
         cp.wait_recv()
@@ -222,15 +222,27 @@
         h = gelu_tanh(jnp.dot(ag[p], win[e], preferred_element_type=F32)).astype(BF16)
         return jnp.dot(h, wout[e], preferred_element_type=F32)
 
+    def mix_copy(h, s, r, dev):
+        return rcopy(
+            snd4.at[r, group_at(s), h], rcv4.at[h, s, r], sem_4.at[0, h, s, r], sem_4.at[1, h, s, r], dev
+        )
+
     def flush(rs):
         for r in rs:
             rcopy(snd3.at[r], rcv3.at[r], sem_3.at[0, r], sem_3.at[1, r], partner).wait_recv()
             y = (keep[r] + rcv3[r].astype(F32)).astype(BF16)
             for q in range(n_exp):
-                snd4[r, q] = y[:, q * cols:(q + 1) * cols]
+                for h in range(n_cut):
+                    low = q * cols + h * wide_cut
+                    snd4[r, q, h] = y[:, low:low + wide_cut]
             for s in range(n_exp):
                 if r or s:
-                    go(rcopy(snd4.at[r, group_at(s)], rcv4.at[s, r], sem_4.at[0, s, r], sem_4.at[1, s, r], across(r, s)))
+                    go(mix_copy(0, s, r, across(r, s)))
+        for h in range(1, n_cut):
+            for r in rs:
+                for s in range(n_exp):
+                    if r or s:
+                        go(mix_copy(h, s, r, across(r, s)))
 
     group = 4
     ready = None
@@ -254,55 +266,40 @@
             flush(ready)
         ready = rs
     flush(ready)
-    for s in range(n_exp):
-        sums = snd4[0, mine].astype(F32) if s == 0 else None
+    every = pl.ds(0, n_exp)
+
+    def so_copy(h, p, sems, r, dev):
+        span = so.at[h, every, p]
+        return rcopy(span, span, sems.at[0, h, r], sems.at[1, h, r], dev)
+
+    for h in range(n_cut):
+        for s in range(n_exp):
+            sums = snd4[0, mine, h].astype(F32) if s == 0 else None
+            for r in range(n_chip):
+                if r or s:
+                    mix_copy(h, s, r, partner).wait_recv()
+                    got = rcv4[h, s, r].astype(F32)
+                    sums = got if sums is None else sums + got
+            so[h, s, piece] = sums.astype(BF16)
+        go(so_copy(h, piece, sem_af, 0, partner))
+        for r in range(1, n_chip):
+            go(so_copy(h, piece, sem_a, r, peer(r)))
+    for h in range(n_cut):
+        for r in range(1, n_chip):
+            p = core * n_chip + near(r)
+            so_copy(h, p, sem_a, r, partner).wait_recv()
+            go(so_copy(h, p, sem_af, r, partner))
+    flat = (n_exp * slots, wide_cut)
+    for h in range(n_cut):
         for r in range(n_chip):
-            if r or s:
-                rcopy(snd4.at[0, 0], rcv4.at[s, r], sem_4.at[0, s, r], sem_4.at[1, s, r], partner).wait_recv()
-                got = rcv4[s, r].astype(F32)
-                sums = got if sums is None else sums + got
-        so[s, piece] = sums.astype(BF16)
-
-    every = pl.ds(0, n_exp)
-
-    def so_copy(p, sems, r, dev):
-        return rcopy(so.at[every, p], so.at[every, p], sems.at[0, r], sems.at[1, r], dev)
-
-    go(so_copy(piece, sem_af, 0, partner))
-    for r in range(1, n_chip):
-        go(so_copy(piece, sem_a, r, peer(r)))
-    for r in range(1, n_chip):
-        p = core * n_chip + near(r)
-        so_copy(p, sem_a, r, partner).wait_recv()
-        go(so_copy(p, sem_af, r, partner))
-    for r in range(n_chip):
-        so_copy(other * n_chip + near(r), sem_af, r, partner).wait_recv()
-    so_out = pltpu.make_async_copy(so, so_hbm, sem_out.at[1])
-    so_out.start()
+            so_copy(h, other * n_chip + near(r), sem_af, r, partner).wait_recv()
+        for i in range(count // step):
+            here = pl.ds(i * step, step)
+            table = so[h].reshape(flat) if rows % 16 == 0 else so[h].astype(F32).reshape(flat).astype(BF16)
+            mixed = jnp.dot(comb[here, :], table, preferred_element_type=F32).astype(BF16)
+            out[here, h * wide_cut:(h + 1) * wide_cut] = mixed
     for cp in pending:
         cp.wait_send()
-    comb_out.wait()
-    so_out.wait()
-
-
-def mix_kernel(comb, so, out):
-    out[...] = jnp.dot(comb[...], so[...], preferred_element_type=F32).astype(BF16)
-
-
-def mix(comb, so):
-    count, slots = comb.shape
-    cols = so.shape[1]
-    step = next(s for s in (384, 256, 128, 64, 32, 16) if count % s == 0)
-    return pl.pallas_call(
-        mix_kernel,
-        out_shape=jax.ShapeDtypeStruct((count, cols), BF16),
-        grid=(count // step,),
-        in_specs=[
-            pl.BlockSpec((step, slots), lambda i: (i, 0)),
-            pl.BlockSpec((slots, cols), lambda i: (0, 0)),
-        ],
-        out_specs=pl.BlockSpec((step, cols), lambda i: (i, 0)),
-    )(comb, so)
 
 
 def solution(mesh):
@@ -318,17 +315,15 @@
         half = slots // 2
         cols = features // n_exp
         n_tile = features // 256
+        n_cut = 2 if cols % 256 == 0 else 1
         dma = pltpu.SemaphoreType.DMA
         vmem = pltpu.VMEM
-        anywhere = pl.BlockSpec(memory_space=pl.ANY)
-        comb, so = pl.pallas_call(
+        anywhere = pl.BlockSpec(memory_space=pltpu.HBM)
+        return pl.pallas_call(
             functools.partial(kernel, n_seq, n_exp, slot_exp),
-            out_shape=(
-                jax.ShapeDtypeStruct((count, n_exp * slots), BF16),
-                jax.ShapeDtypeStruct((n_exp, n_seq, rows, cols), BF16),
-            ),
+            out_shape=jax.ShapeDtypeStruct((count, cols), BF16),
             in_specs=[anywhere] * 4,
-            out_specs=(anywhere, anywhere),
+            out_specs=pl.BlockSpec(memory_space=pltpu.VMEM),
             scratch_shapes=[
                 vmem((count, features), BF16),
                 vmem((n_exp, features, slots), BF16),
@@ -352,12 +347,11 @@
                 vmem((n_chip, rows, features), F32),
                 vmem((n_chip, rows, features), BF16),
                 vmem((n_chip, rows, features), BF16),
-                vmem((n_chip, n_exp, rows, cols), BF16),
-                vmem((n_exp, n_chip, rows, cols), BF16),
-                vmem((n_exp, n_seq, rows, cols), BF16),
+                vmem((n_chip, n_exp, n_cut, rows, cols // n_cut), BF16),
+                vmem((n_cut, n_exp, n_chip, rows, cols // n_cut), BF16),
+                vmem((n_cut, n_exp, n_seq, rows, cols // n_cut), BF16),
                 dma((-(-count // 512),)),
                 dma,
-                dma((2,)),
                 dma((2,)),
                 dma((2, n_exp)),
                 dma((2, n_exp)),
@@ -368,16 +362,14 @@
                 dma((2, n_chip)),
                 dma((2, n_chip)),
                 dma((2, n_chip)),
-                dma((2, n_exp, n_chip)),
-                dma((2, n_chip)),
-                dma((2, n_chip)),
+                dma((2, n_cut, n_exp, n_chip)),
+                dma((2, n_cut, n_chip)),
+                dma((2, n_cut, n_chip)),
             ],
             compiler_params=pltpu.CompilerParams(
-                collective_id=0, has_side_effects=True, vmem_limit_bytes=60 * 1024 * 1024
+                collective_id=0, has_side_effects=True, vmem_limit_bytes=49 * 1024 * 1024
             ),
         )(tokens, slot_embed, w_in, w_out)
-        so = so.reshape(n_exp * slots, cols)
-        return mix(comb, so)
 
     placed = (P("seq", None), P(None, "exp"), P("exp", None, "seq"), P("exp", "seq", None))
     return jax.shard_map(

time: 54.4 us -> 50.5 us (0.928); the launches traced: 53.5 us -> 50.3 us
  Pallas kernels: 53.5 us -> 48 us
  local copies, waits for them, and re-layouts: 0 us -> 2.32 us
    pallas_call x1 -> x0, Pallas kernels: 5.35 us -> none  [mix(): pl.pallas_call(mix_kernel, out_shape=jax.ShapeDtypeStruct((count, cols),...]
    unnamed x0 -> x3, local copies, waits for them, and re-layouts: none -> 2.32 us
where the time goes in v3:
time: 50.5 us; the launch traced here: 50.3 us
  Pallas kernels  48 us (95%)
  local copies, waits for them, and re-layouts  2.32 us (5%)
    pallas_call x1, Pallas kernels, on_device(): pl.pallas_call(functools.partial(kernel, n_seq, n_exp, slot_exp), out_sha...  48 us
    unnamed x3, local copies, waits for them, and re-layouts  2.32 us

profile of v3, /device:TPU:0, one launch (start us, length us, event | category | flops | bytes accessed | tf_op | source)
XLA Modules:
  0.0 50.3 jit_solution(4649264545971887562)
XLA Ops:
  0.0 0.0 copy-start
  0.0 1.0 %copy-done = bf16[1024,256]{1,0:T(8,128)(2,1)S(1)} copy-done((bf16[1024,256]{1,0:T(8,128)(2,1)S(1)}, bf16[1024,256]{1,0:T(8,128)(2,1)}, u32[]{:S(2)}) %copy-start) | copy-done | bytes 524312
  1.0 48.0 %shard_map.46 = bf16[1920,512]{1,0:T(8,128)(2,1)S(1)} custom-call(bf16[1920,1024]{1,0:T(8,128)(2,1)} %tok_hbm.1, bf16[1024,256]{1,0:T(8,128)(2,1)S(1)} %copy-done, bf16[16,1024,256]{2,1,0:T(8,128)(2,1)} %win_hbm.1, bf16[16,256,1024]{2,1,0:T(8,128)(2,1)} %wout_hbm.1), custom_call_target="tpu_custom_call" | custom-call | tf_op jit(solution)/shard_map/pallas_call | solution.py:322
  49.1 1.3 %copy.6 = bf16[1920,512]{1,0:T(8,128)(2,1)} copy(bf16[1920,512]{1,0:T(8,128)(2,1)S(1)} %shard_map.46) | data formatting | bytes 3932160
Async XLA Ops:
  0.0 1.0 %copy-start = (bf16[1024,256]{1,0:T(8,128)(2,1)S(1)}, bf16[1024,256]{1,0:T(8,128)(2,1)}, u32[]{:S(2)}) copy-start(bf16[1024,256]{1,0:T(8,128)(2,1)} %emb_hbm.1) | copy-start | bytes 1572868

commit v4 on v3

--- a/solution.py
+++ b/solution.py
@@ -244,7 +244,7 @@
                     if r or s:
                         go(mix_copy(h, s, r, across(r, s)))
 
-    group = 4
+    group = 2
     ready = None
     for start in range(0, n_chip, group):
         rs = range(start, min(start + group, n_chip))

time: 50.5 us -> 51.6 us (1.022)
  Pallas kernels: 48 us -> 49.2 us
    pallas_call x1, Pallas kernels: 48 us -> 49.2 us  [on_device(): pl.pallas_call(functools.partial(kernel, n_seq, n_exp, slot_exp), out_sha...]
where the time goes in v4:
time: 51.6 us; the launch traced here: 51.5 us
  Pallas kernels  49.2 us (95%)
  local copies, waits for them, and re-layouts  2.32 us (4%)
    pallas_call x1, Pallas kernels, on_device(): pl.pallas_call(functools.partial(kernel, n_seq, n_exp, slot_exp), out_sha...  49.2 us
    unnamed x3, local copies, waits for them, and re-layouts  2.32 us

profile of v4, /device:TPU:0, one launch (start us, length us, event | category | flops | bytes accessed | tf_op | source)
XLA Modules:
  0.0 51.5 jit_solution(10140687583325273299)
XLA Ops:
  0.0 0.0 copy-start
  0.0 1.0 %copy-done = bf16[1024,256]{1,0:T(8,128)(2,1)S(1)} copy-done((bf16[1024,256]{1,0:T(8,128)(2,1)S(1)}, bf16[1024,256]{1,0:T(8,128)(2,1)}, u32[]{:S(2)}) %copy-start) | copy-done | bytes 524312
  1.0 49.2 %shard_map.46 = bf16[1920,512]{1,0:T(8,128)(2,1)S(1)} custom-call(bf16[1920,1024]{1,0:T(8,128)(2,1)} %tok_hbm.1, bf16[1024,256]{1,0:T(8,128)(2,1)S(1)} %copy-done, bf16[16,1024,256]{2,1,0:T(8,128)(2,1)} %win_hbm.1, bf16[16,256,1024]{2,1,0:T(8,128)(2,1)} %wout_hbm.1), custom_call_target="tpu_custom_call" | custom-call | tf_op jit(solution)/shard_map/pallas_call | solution.py:322
  50.2 1.3 %copy.6 = bf16[1920,512]{1,0:T(8,128)(2,1)} copy(bf16[1920,512]{1,0:T(8,128)(2,1)S(1)} %shard_map.46) | data formatting | bytes 3932160
Async XLA Ops:
  0.0 1.0 %copy-start = (bf16[1024,256]{1,0:T(8,128)(2,1)S(1)}, bf16[1024,256]{1,0:T(8,128)(2,1)}, u32[]{:S(2)}) copy-start(bf16[1024,256]{1,0:T(8,128)(2,1)} %emb_hbm.1) | copy-start | bytes 1572868
